TPU v7x, 32 devices: a whole 2x2x4 slice. The times are simulated.
32 devices in a mesh: blk: 8 (over z, y), rep: 4 (over x, core).
Axes of the slice: x: 2, y: 2, z: 4, core: 2. Of those that a mesh axis runs over, the one named last changes fastest.
Arguments:
- features: bfloat16 [8192, 256], P(('blk', 'rep')), may hold values from -6 to 6
- tiles: bfloat16 [8, 64, 128, 128], P('blk', 'rep'), may hold values from -0.25 to 0.25
- tile_rows: int32 [8, 64], P('blk', 'rep'), may hold values from 0 to 7
- tile_cols: int32 [8, 64], P('blk', 'rep'), may hold values from 0 to 15
- counts: int32 [8, 4], P('blk', 'rep'), may hold values from 4 to 16
- weight: bfloat16 [256, 256], replicated, may hold values from -0.375 to 0.375
- bias: float32 [256], replicated, may hold values from -3 to 3
- cotangent: bfloat16 [8192, 256], P(('blk', 'rep')), may hold values from -6 to 6
Outputs:
- activations: bfloat16 [8192, 256], P(('blk', 'rep'))
- feature_grad: bfloat16 [8192, 256], P(('blk', 'rep'))
- weight_grad: float32 [256, 256], replicated
- bias_grad: float32 [256], replicated
All inputs are finite; a program needn't handle non-finite values.
Results may differ from a plain program's by a relative error of at most 0.006.
Values may be sent and summed in bfloat16 or wider, within the bound.
A program may use at most 64 MiB of HBM per device.

v0:
```python
import jax
import jax.numpy as jnp
from jax import lax
from jax.sharding import PartitionSpec as P


def shifted(block, axis, distance):
    devices = range(lax.axis_size(axis))
    route = [((i - distance) % len(devices), i) for i in devices]
    return lax.ppermute(block, axis, route)


def per_device(features, tiles, tile_rows, tile_cols, counts, weight, bias, cotangent):
    highest = lax.Precision.HIGHEST
    tile_size = tiles.shape[2]
    slot_count = tiles.shape[1]
    feat_width = features.shape[1]
    own_rows = features.shape[0]
    own_tiles = own_rows // tile_size
    rep_count = lax.axis_size("rep")
    blk_count = lax.axis_size("blk")
    slot_tiles = tiles[0]
    row_index = tile_rows[0]
    col_index = tile_cols[0]
    slot_live = (jnp.arange(slot_count, dtype=jnp.int32) < counts[0, 0]).astype(jnp.float32)
    wanted = col_index[:, None] * tile_size + jnp.arange(tile_size, dtype=jnp.int32)[None, :]
    piece = lax.all_gather(features, "blk", axis=0, tiled=True)
    piece_count = piece.shape[0]
    inside = (wanted >= 0) & (wanted < piece_count)
    clipped = jnp.clip(wanted, 0, piece_count - 1)
    taken = jnp.take(piece, clipped.reshape(-1), axis=0).reshape(slot_count, tile_size, feat_width)
    selected = jnp.where(inside[:, :, None], taken, jnp.zeros((), jnp.bfloat16))
    partial_value = jnp.einsum(
        "sij,sjf->sif", slot_tiles, selected, preferred_element_type=jnp.float32
    )
    row_onehot = (
        row_index[:, None] == jnp.arange(rep_count * own_tiles, dtype=jnp.int32)[None, :]
    ).astype(jnp.float32) * slot_live[:, None]
    summed = jnp.einsum("st,sif->tif", row_onehot, partial_value, precision=highest)
    aggregate = lax.psum_scatter(
        summed.reshape(rep_count * own_rows, feat_width), "rep", scatter_dimension=0, tiled=True
    ).astype(jnp.bfloat16)
    pre_act = jnp.dot(aggregate, weight, preferred_element_type=jnp.float32) + bias[None, :]
    logistic = jax.nn.sigmoid(pre_act)
    activations = (pre_act * logistic).astype(jnp.bfloat16)
    act_grad = (
        cotangent.astype(jnp.float32) * logistic * (1.0 + pre_act * (1.0 - logistic))
    ).astype(jnp.bfloat16)
    local_weight = jnp.dot(aggregate.T, act_grad, preferred_element_type=jnp.float32)
    local_bias = jnp.sum(act_grad.astype(jnp.float32), axis=0)
    weight_grad, bias_grad = lax.psum((local_weight, local_bias), ("blk", "rep"))
    scale_factor = 1.0 / (blk_count * rep_count)
    weight_grad = weight_grad * scale_factor
    bias_grad = bias_grad * scale_factor
    agg_grad = jnp.dot(act_grad, weight.T, preferred_element_type=jnp.float32).astype(jnp.bfloat16)
    gathered = lax.all_gather(agg_grad, "rep", axis=0, tiled=True).reshape(
        rep_count * own_tiles, tile_size, feat_width
    )
    chosen = jnp.take(gathered, row_index, axis=0)
    contribution = (
        jnp.einsum("sij,sif->sjf", slot_tiles, chosen, preferred_element_type=jnp.float32)
        * slot_live[:, None, None]
    )

    def column_terms(first_row, row_count):
        targets = first_row // tile_size + jnp.arange(row_count // tile_size, dtype=jnp.int32)
        col_onehot = (col_index[:, None] == targets[None, :]).astype(jnp.float32)
        placed = jnp.einsum("sp,sjf->pjf", col_onehot, contribution, precision=highest)
        return placed.reshape(row_count, feat_width)

    own_block = lax.axis_index("blk")

    def travel_step(step_index, travelling):
        source_block = (own_block - step_index) % blk_count
        travelling = travelling + column_terms(source_block * own_rows, own_rows)
        return shifted(travelling, "blk", 1)

    feature_sum = lax.fori_loop(
        0, blk_count, travel_step, jnp.zeros((own_rows, feat_width), jnp.float32)
    )
    feature_grad = feature_sum.astype(jnp.bfloat16)
    return (activations, feature_grad, weight_grad, bias_grad)


def solution(mesh):
    in_specs = (
        P(("blk", "rep"), None),
        P("blk", "rep", None, None),
        P("blk", "rep"),
        P("blk", "rep"),
        P("blk", "rep"),
        P(),
        P(),
        P(("blk", "rep"), None),
    )
    out_specs = (P(("blk", "rep"), None), P(("blk", "rep"), None), P(), P())
    return jax.shard_map(
        per_device, mesh=mesh, in_specs=in_specs, out_specs=out_specs, check_vma=False
    )
```

profile of v0, /device:TPU:0, one launch (start us, length us, event | category | flops | bytes accessed | tf_op | source)
XLA Modules:
  0.0 242.2 jit_solution(17766153802447288838)
XLA Ops:
  9.5 43.7 %all-gather.2.cloned.1.call-done = bf16[2048,256]{1,0:T(8,128)(2,1)} async-done(((bf16[256,256]{1,0:T(8,128)(2,1)}), bf16[2048,256]{1,0:T(8,128)(2,1)}) %all-gather.2.cloned.1.call-update) | async-done | bytes 1048592 | tf_op jit(solution)/shard_map/all_gather | solution.py:27
  53.1 9.8 %gather_fusion = bf16[2048,256]{1,0:T(8,128)(2,1)} fusion(bf16[2048,256]{1,0:T(8,128)(2,1)} %all-gather.2.cloned.1.call-done, s32[2048]{0:T(1024)S(1)} %broadcast_clamp_fusion), kind=kCustom, calls=%fused_computation | custom fusion | bytes 2105344 | tf_op jit(solution)/shard_map/jit(_take)/gather | solution.py:31
  63.0 2.3 fusion.8
  65.3 2.1 copy.18
  67.4 2.7 %fusion.5 = f32[8,128,256]{2,0,1:T(8,128)S(1)} fusion(f32[16,256,128]{1,0,2:T(8,128)} %copy.18, f32[16]{0:T(128)S(1)} %compare_convert_fusion, s32[16]{0:T(128)S(1)} %bitcast.53), kind=kOutput, calls=%fused_computation.9 | convolution fusion | flops 50331904 | bytes 3145856 | tf_op jit(solution)/shard_map/st,sif->tif/dot_general | solution.py:39
  70.2 1.3 copy.15
  71.6 23.6 %reduce-scatter.2.cloned.1.call-done = f32[256,256]{1,0:T(8,128)} async-done(((f32[1024,256]{1,0:T(8,128)}), f32[256,256]{1,0:T(8,128)}) %reduce-scatter.2.cloned.1.call-update) | async-done | bytes 262160 | tf_op jit(solution)/shard_map/reduce_scatter | solution.py:40
  95.2 2.0 convert_reduce_fusion
  97.4 0.9 fusion.19
  98.3 6.6 %all_gather.7 = bf16[1024,256]{1,0:T(8,128)(2,1)S(1)} all-gather(bf16[256,256]{1,0:T(8,128)(2,1)S(1)} %convolution_convert_fusion), channel_id=1, replica_groups=mesh['blk'=8,'rep'=4] {'rep'}, dimensions={0}, use_global_device_ids=true | all-gather | bytes 655360 | tf_op jit(solution)/shard_map/all_gather | solution.py:56
  105.6 1.9 multiply_bitcast_fusion
  107.5 2.2 copy.17
  109.8 86.1 %while.15 = (s32[]{:T(128)}, f32[256,256]{1,0:T(8,128)S(1)}, s32[1,16]{1,0:T(1,128)S(1)}, s32[]{:T(128)}, f32[16,128,256]{2,0,1:T(8,128)S(1)}, /*index=5*/s32[]{...) while((s32[]{:T(128)}, f32[256,256]{1,0:T(8,128)S(1)}, ...), condition=%wide.region_2.3_spmd, body=%wide.region_1.2_spmd.sunk | while | flops 12648512 | bytes 4719116 | solution.py:78
  109.8 0.8 fusion.46
  110.7 1.5 collective-permute-start
  112.3 10.2 %collective-permute-done = f32[256,256]{1,0:T(8,128)S(1)} collective-permute-done((f32[256,256]{1,0:T(8,128)S(1)}, f32[256,256]{1,0:T(8,128)S(1)}, u32[]{:S(2)}, u32[]{:S(2)}) %collective-permute-start) | collective-permute-done | bytes 262176 | tf_op jit(solution)/shard_map/while/body/eval_jaxpr/ppermute | solution.py:10
  122.4 0.8 fusion.46
  123.4 10.6 %collective-permute-done = f32[256,256]{1,0:T(8,128)S(1)} collective-permute-done((f32[256,256]{1,0:T(8,128)S(1)}, f32[256,256]{1,0:T(8,128)S(1)}, u32[]{:S(2)}, u32[]{:S(2)}) %collective-permute-start) | collective-permute-done | bytes 262176 | tf_op jit(solution)/shard_map/while/body/eval_jaxpr/ppermute | solution.py:10
  134.0 0.8 fusion.46
  135.0 9.8 %collective-permute-done = f32[256,256]{1,0:T(8,128)S(1)} collective-permute-done((f32[256,256]{1,0:T(8,128)S(1)}, f32[256,256]{1,0:T(8,128)S(1)}, u32[]{:S(2)}, u32[]{:S(2)}) %collective-permute-start) | collective-permute-done | bytes 262176 | tf_op jit(solution)/shard_map/while/body/eval_jaxpr/ppermute | solution.py:10
  144.7 0.8 fusion.46
  145.7 9.1 %collective-permute-done = f32[256,256]{1,0:T(8,128)S(1)} collective-permute-done((f32[256,256]{1,0:T(8,128)S(1)}, f32[256,256]{1,0:T(8,128)S(1)}, u32[]{:S(2)}, u32[]{:S(2)}) %collective-permute-start) | collective-permute-done | bytes 262176 | tf_op jit(solution)/shard_map/while/body/eval_jaxpr/ppermute | solution.py:10
  154.8 0.8 fusion.46
  155.7 9.2 %collective-permute-done = f32[256,256]{1,0:T(8,128)S(1)} collective-permute-done((f32[256,256]{1,0:T(8,128)S(1)}, f32[256,256]{1,0:T(8,128)S(1)}, u32[]{:S(2)}, u32[]{:S(2)}) %collective-permute-start) | collective-permute-done | bytes 262176 | tf_op jit(solution)/shard_map/while/body/eval_jaxpr/ppermute | solution.py:10
  164.9 0.8 fusion.46
  165.9 9.1 %collective-permute-done = f32[256,256]{1,0:T(8,128)S(1)} collective-permute-done((f32[256,256]{1,0:T(8,128)S(1)}, f32[256,256]{1,0:T(8,128)S(1)}, u32[]{:S(2)}, u32[]{:S(2)}) %collective-permute-start) | collective-permute-done | bytes 262176 | tf_op jit(solution)/shard_map/while/body/eval_jaxpr/ppermute | solution.py:10
  175.0 0.8 fusion.46
  175.9 9.8 %collective-permute-done = f32[256,256]{1,0:T(8,128)S(1)} collective-permute-done((f32[256,256]{1,0:T(8,128)S(1)}, f32[256,256]{1,0:T(8,128)S(1)}, u32[]{:S(2)}, u32[]{:S(2)}) %collective-permute-start) | collective-permute-done | bytes 262176 | tf_op jit(solution)/shard_map/while/body/eval_jaxpr/ppermute | solution.py:10
  185.8 0.8 fusion.46
  186.7 9.2 %collective-permute-done = f32[256,256]{1,0:T(8,128)S(1)} collective-permute-done((f32[256,256]{1,0:T(8,128)S(1)}, f32[256,256]{1,0:T(8,128)S(1)}, u32[]{:S(2)}, u32[]{:S(2)}) %collective-permute-start) | collective-permute-done | bytes 262176 | tf_op jit(solution)/shard_map/while/body/eval_jaxpr/ppermute | solution.py:10
  196.5 36.9 %psum.15 = f32[256]{0:T(256)S(1)} all-reduce(f32[256]{0:T(256)S(1)} %get-tuple-element.160), channel_id=1, replica_groups=mesh['blk'=8,'rep'=4] {'blk','rep'}, use_global_device_ids=true, to_apply=%region_5.6 | all-reduce | flops 256 | bytes 2048 | tf_op jit(solution)/shard_map/psum | solution.py:51
  234.0 1.7 broadcast_multiply_fusion
  (66 shorter events, 4.7 us)
Async XLA Ops:
  7.2 55.8 %copy-start = (bf16[1,16,128,128]{3,2,1,0:T(8,128)(2,1)S(1)}, bf16[1,16,128,128]{3,2,1,0:T(8,128)(2,1)}, u32[]{:S(2)}) copy-start(bf16[1,16,128,128]{3,2,1,0:T(8,128)(2,1)} %param.11) | copy-start | bytes 1572868
  7.2 46.0 %all-gather.2.cloned.1.call-start = ((), (), s32[]{:S(2)}) async-start(), calls=%async_computation.1 | async-start | bytes 1179648 | tf_op jit(solution)/shard_map/all_gather | solution.py:27
  7.9 87.2 %reduce-scatter.2.cloned.1.call-start = ((), (), s32[]{:S(2)}) async-start(), calls=%async_computation.2 | async-start | bytes 1310720 | tf_op jit(solution)/shard_map/reduce_scatter | solution.py:40
  65.3 2.1 copy-start.4
  70.1 25.0 %copy-start.2 = (bf16[256,256]{1,0:T(8,128)(2,1)S(1)}, bf16[256,256]{1,0:T(8,128)(2,1)}, u32[]{:S(2)}) copy-start(bf16[256,256]{1,0:T(8,128)(2,1)} %param.15) | copy-start | bytes 393220
  70.1 25.0 %copy-start.5 = (bf16[256,256]{1,0:T(8,128)(2,1)S(1)}, bf16[256,256]{1,0:T(8,128)(2,1)}, u32[]{:S(2)}) copy-start(bf16[256,256]{1,0:T(8,128)(2,1)} %param.17) | copy-start | bytes 393220
  70.1 25.0 %copy-start.6 = (f32[256]{0:T(256)S(1)}, f32[256]{0:T(256)}, u32[]{:S(2)}) copy-start(f32[256]{0:T(256)} %param.16) | copy-start | bytes 3076
  71.5 162.5 %all-reduce.2.cloned.1.call-start = ((), (), s32[]{:S(2)}) async-start(), calls=%async_computation.3 | async-start | bytes 524288 | tf_op jit(solution)/shard_map/psum | solution.py:51
  95.2 2.2 copy-start.1
  107.5 2.3 copy-start.3
  110.7 11.7 %collective-permute-start = (f32[256,256]{1,0:T(8,128)S(1)}, f32[256,256]{1,0:T(8,128)S(1)}, u32[]{:S(2)}, u32[]{:S(2)}) collective-permute-start(f32[256,256]{1,0:T(8,128)S(1)} %bitcast_add_fusion.2), channel_id=1, source_target_pairs={{28,0},{0,4},{4,8},{8,12},{12,16},{16,20},{20,24},{24,28},{29,1},{... | collective-permute-start | bytes 786440 | tf_op jit(solution)/shard_map/while/body/eval_jaxpr/ppermute | solution.py:10
  123.3 10.6 %collective-permute-start = (f32[256,256]{1,0:T(8,128)S(1)}, f32[256,256]{1,0:T(8,128)S(1)}, u32[]{:S(2)}, u32[]{:S(2)}) collective-permute-start(f32[256,256]{1,0:T(8,128)S(1)} %bitcast_add_fusion.2), channel_id=1, source_target_pairs={{28,0},{0,4},{4,8},{8,12},{12,16},{16,20},{20,24},{24,28},{29,1},{... | collective-permute-start | bytes 786440 | tf_op jit(solution)/shard_map/while/body/eval_jaxpr/ppermute | solution.py:10
  134.9 9.8 %collective-permute-start = (f32[256,256]{1,0:T(8,128)S(1)}, f32[256,256]{1,0:T(8,128)S(1)}, u32[]{:S(2)}, u32[]{:S(2)}) collective-permute-start(f32[256,256]{1,0:T(8,128)S(1)} %bitcast_add_fusion.2), channel_id=1, source_target_pairs={{28,0},{0,4},{4,8},{8,12},{12,16},{16,20},{20,24},{24,28},{29,1},{... | collective-permute-start | bytes 786440 | tf_op jit(solution)/shard_map/while/body/eval_jaxpr/ppermute | solution.py:10
  145.6 9.1 %collective-permute-start = (f32[256,256]{1,0:T(8,128)S(1)}, f32[256,256]{1,0:T(8,128)S(1)}, u32[]{:S(2)}, u32[]{:S(2)}) collective-permute-start(f32[256,256]{1,0:T(8,128)S(1)} %bitcast_add_fusion.2), channel_id=1, source_target_pairs={{28,0},{0,4},{4,8},{8,12},{12,16},{16,20},{20,24},{24,28},{29,1},{... | collective-permute-start | bytes 786440 | tf_op jit(solution)/shard_map/while/body/eval_jaxpr/ppermute | solution.py:10
  155.7 9.3 %collective-permute-start = (f32[256,256]{1,0:T(8,128)S(1)}, f32[256,256]{1,0:T(8,128)S(1)}, u32[]{:S(2)}, u32[]{:S(2)}) collective-permute-start(f32[256,256]{1,0:T(8,128)S(1)} %bitcast_add_fusion.2), channel_id=1, source_target_pairs={{28,0},{0,4},{4,8},{8,12},{12,16},{16,20},{20,24},{24,28},{29,1},{... | collective-permute-start | bytes 786440 | tf_op jit(solution)/shard_map/while/body/eval_jaxpr/ppermute | solution.py:10
  165.9 9.1 %collective-permute-start = (f32[256,256]{1,0:T(8,128)S(1)}, f32[256,256]{1,0:T(8,128)S(1)}, u32[]{:S(2)}, u32[]{:S(2)}) collective-permute-start(f32[256,256]{1,0:T(8,128)S(1)} %bitcast_add_fusion.2), channel_id=1, source_target_pairs={{28,0},{0,4},{4,8},{8,12},{12,16},{16,20},{20,24},{24,28},{29,1},{... | collective-permute-start | bytes 786440 | tf_op jit(solution)/shard_map/while/body/eval_jaxpr/ppermute | solution.py:10
  175.9 9.9 %collective-permute-start = (f32[256,256]{1,0:T(8,128)S(1)}, f32[256,256]{1,0:T(8,128)S(1)}, u32[]{:S(2)}, u32[]{:S(2)}) collective-permute-start(f32[256,256]{1,0:T(8,128)S(1)} %bitcast_add_fusion.2), channel_id=1, source_target_pairs={{28,0},{0,4},{4,8},{8,12},{12,16},{16,20},{20,24},{24,28},{29,1},{... | collective-permute-start | bytes 786440 | tf_op jit(solution)/shard_map/while/body/eval_jaxpr/ppermute | solution.py:10
  186.7 9.2 %collective-permute-start = (f32[256,256]{1,0:T(8,128)S(1)}, f32[256,256]{1,0:T(8,128)S(1)}, u32[]{:S(2)}, u32[]{:S(2)}) collective-permute-start(f32[256,256]{1,0:T(8,128)S(1)} %bitcast_add_fusion.2), channel_id=1, source_target_pairs={{28,0},{0,4},{4,8},{8,12},{12,16},{16,20},{20,24},{24,28},{29,1},{... | collective-permute-start | bytes 786440 | tf_op jit(solution)/shard_map/while/body/eval_jaxpr/ppermute | solution.py:10
Sparse Core Ops, SparseCore 0:
  10.1 42.9 all-gather.1
  71.6 23.5 reduce-scatter.1
  101.2 130.9 all-reduce.1
where the time goes:
time: 243 us; the launch traced here: 242 us
  waiting for transfers between devices  145 us (60%)
  blocking collectives  43.5 us (18%)
  matrix products  16.7 us (7%)
  local copies, waits for them, and re-layouts  16.3 us (7%)
  between operations  14.6 us (6%)
  other arithmetic  4.1 us (2%)
    ppermute x8, waiting for transfers between devices, shifted(): return lax.ppermute(block, axis, route)  76.8 us
    all_gather x1, waiting for transfers between devices, per_device(): piece = lax.all_gather(features, 'blk', axis=0, tiled=True)  43.7 us
    psum x1, blocking collectives, per_device(): lax.psum((local_weight, local_bias), ('blk', 'rep'))  36.9 us
    reduce_scatter x1, waiting for transfers between devices, per_device(): lax.psum_scatter(summed.reshape(rep_count * own_rows, feat_width), 'rep',...  23.6 us
    gather x1, local copies, waits for them, and re-layouts, per_device(): jnp.take(piece, clipped.reshape(-1), axis=0)  9.83 us
    all_gather x1, blocking collectives, per_device(): lax.all_gather(agg_grad, 'rep', axis=0, tiled=True)  6.61 us
    dot_general x8, matrix products, column_terms(): jnp.einsum('sp,sjf->pjf', col_onehot, contribution, precision=highest)  6.57 us
  transfers between devices with their start and end apart: 11, of which 10 were waited for; matrix products, arithmetic and copies ran while one was open for 6% of the time, Pallas kernels for 0%

commit v1 on v0

v1 whole, which is shorter than its diff:
```python
import functools

import jax
import jax.numpy as jnp
from jax import lax
from jax.experimental import pallas as pl
from jax.experimental.pallas import tpu as pltpu
from jax.sharding import PartitionSpec as P

MESH = pl.DeviceIdType.MESH
F32 = jnp.float32
BF16 = jnp.bfloat16


def flip(index, bits):
    out = index
    bit = 1
    while bit <= bits:
        if bits & bit:
            out = out + bit - 2 * bit * ((index // bit) % 2)
        bit *= 2
    return out


def kernel(n, R, T, S, features, tiles, rows, cols, counts, weight, bias, cotangent,
           act_out, fgrad_out, wgrad_out, bgrad_out,
           feat, tile_v, weight_v, cot_v, prod, send_b, recv_b, grads,
           send_d1, recv_d1, send_d2, recv_d2,
           send_w1, recv_w1, send_w2, recv_w2, slab_w3, slab_w4,
           load_sem, az_send, az_recv, ay_send, ay_recv, b_send, b_recv, c_send, c_recv,
           d1_send, d1_recv, d2_send, d2_recv, w1_send, w1_recv, w2_send, w2_recv,
           w3_send, w3_recv, w4_send, w4_recv):
    b = lax.axis_index("blk")
    r = lax.axis_index("rep")
    half = n // 2
    size = tiles.shape[1]
    width = weight.shape[1]
    fr = send_w1.shape[1] - 8
    fb = fr // n
    cb = send_w2.shape[1] - 8
    partner = flip(b, 1)

    def remote(src, dst, ssem, rsem, device):
        return pltpu.make_async_remote_copy(
            src_ref=src, dst_ref=dst, send_sem=ssem, recv_sem=rsem,
            device_id=device, device_id_type=MESH)

    loads = [
        pltpu.make_async_copy(features, feat.at[pl.ds(b * T, T)], load_sem.at[0]),
        pltpu.make_async_copy(tiles, tile_v, load_sem.at[1]),
        pltpu.make_async_copy(weight, weight_v, load_sem.at[2]),
        pltpu.make_async_copy(cotangent, cot_v, load_sem.at[3]),
    ]
    for c in loads:
        c.start()

    barrier = pltpu.get_barrier_semaphore()
    for s in range(1, n):
        pl.semaphore_signal(barrier, inc=1, device_id=(flip(b, s), r), device_id_type=MESH)
    for s in range(1, R):
        pl.semaphore_signal(barrier, inc=1, device_id=(b, flip(r, s)), device_id_type=MESH)
    pl.semaphore_wait(barrier, n - 1 + R - 1)

    mine = feat.at[pl.ds(b * T, T)]
    loads[0].wait()
    az = [None] * half
    order = sorted(range(1, half), key=lambda q: (q.bit_count(), q))
    ay = [None] * half
    ay[0] = remote(mine, mine, ay_send.at[0], ay_recv.at[0], (partner, r))
    ay[0].start()
    for q in order:
        az[q] = remote(mine, mine, az_send.at[q], az_recv.at[q], (flip(b, 2 * q), r))
        az[q].start()
    for q in order:
        az[q].wait_recv()
        block = feat.at[pl.ds(flip(b, 2 * q) * T, T)]
        ay[q] = remote(block, block, ay_send.at[q], ay_recv.at[q], (partner, r))
        ay[q].start()
    loads[1].wait()
    for q in [0] + order:
        ay[q].wait_recv()

    live = [lax.convert_element_type(k < counts[0, 0], F32) for k in range(S)]
    row_of = [rows[0, k] for k in range(S)]
    col_of = [cols[0, k] for k in range(S)]

    for k in range(S):
        prod[k] = jnp.dot(tile_v[k], feat[col_of[k]], preferred_element_type=F32)

    step = 32

    def combine(index_of, target, dest):
        w = [jnp.where(index_of[k] == target, live[k], 0.0) for k in range(S)]

        def chunk(i, carry):
            at = pl.multiple_of(i * step, step)
            total = prod[0, pl.ds(at, step), :] * w[0]
            for k in range(1, S):
                total = total + prod[k, pl.ds(at, step), :] * w[k]
            dest(at, total)
            return carry

        lax.fori_loop(0, size // step, chunk, 0)

    bs = {}
    peers = sorted(range(1, R), key=lambda s: (-(s // 2), s))
    for s in peers:
        peer = flip(r, s)
        for t in range(T):
            def put(at, value, t=t, s=s):
                send_b[s, t, pl.ds(at, step), :] = value.astype(BF16)
            combine(row_of, peer * T + t, put)
        bs[s] = remote(send_b.at[s], recv_b.at[s], b_send.at[s], b_recv.at[s], (b, peer))
        bs[s].start()
    own_value = []
    for t in range(T):
        w = [jnp.where(row_of[k] == r * T + t, live[k], 0.0) for k in range(S)]
        total = prod[0] * w[0]
        for k in range(1, S):
            total = total + prod[k] * w[k]
        own_value.append(total)
    total = jnp.concatenate(own_value, axis=0)
    loads[2].wait()
    loads[3].wait()
    for s in peers[::-1]:
        bs[s].wait_recv()
        total = total + recv_b[s].reshape(T * size, width).astype(F32)
    agg = total.astype(BF16)
    pre = jnp.dot(agg, weight_v[...], preferred_element_type=F32) + bias[...]
    sig = jax.nn.sigmoid(pre)
    act_grad = (cot_v[...].astype(F32) * sig * (1.0 + pre * (1.0 - sig))).astype(BF16)
    grad = lax.dot_general(act_grad, weight_v[...], (((1,), (1,)), ((), ())),
                           preferred_element_type=F32).astype(BF16)
    here = grads.at[pl.ds(r * T, T)]
    grads[pl.ds(r * T, T)] = grad.reshape(T, size, width)
    cs = {}
    for s in peers:
        cs[s] = remote(here, here, c_send.at[s], c_recv.at[s], (b, flip(r, s)))
        cs[s].start()

    act_out[...] = (pre * sig).astype(BF16)
    part = lax.dot_general(agg, act_grad, (((0,), (0,)), ((), ())), preferred_element_type=F32)
    bias_part = jnp.sum(act_grad.astype(F32).reshape(-1, 8, width), axis=0)
    for q in range(R):
        send_w1[q, :fr, :] = part[q * fr:(q + 1) * fr, :]
        send_w1[q, fr:, :] = bias_part
    w1 = {}
    for s in peers:
        peer = flip(r, s)
        w1[s] = remote(send_w1.at[peer], recv_w1.at[r], w1_send.at[s], w1_recv.at[s], (b, peer))
        w1[s].start()
    recv_w1[r] = send_w1[r]

    for s in peers:
        cs[s].wait_recv()
    for k in range(S):
        prod[k] = lax.dot_general(tile_v[k], grads[row_of[k]], (((0,), (0,)), ((), ())),
                                  preferred_element_type=F32)

    far = order[::-1]
    d1 = {}
    for q in far + [0]:
        goal = flip(partner, 2 * q)
        for t in range(T):
            def put(at, value, t=t, q=q):
                send_d1[q, t, pl.ds(at, step), :] = value.astype(BF16)
            combine(col_of, goal * T + t, put)
        d1[q] = remote(send_d1.at[q], recv_d1.at[q], d1_send.at[q], d1_recv.at[q], (partner, r))
        d1[q].start()

    for s in peers:
        w1[s].wait_recv()
    summed = recv_w1[0]
    for q in range(1, R):
        summed = summed + recv_w1[q]
    for j in range(n):
        send_w2[j, :fb, :] = summed[j * fb:(j + 1) * fb, :]
        send_w2[j, cb:, :] = summed[fr:, :]
    w2 = {}
    for s in range(1, n):
        peer = flip(b, s)
        w2[s] = remote(send_w2.at[peer], recv_w2.at[b], w2_send.at[s], w2_recv.at[s], (peer, r))
        w2[s].start()
    recv_w2[b] = send_w2[b]

    d2 = {}
    for q in far:
        goal = flip(b, 2 * q)
        d1[q].wait_recv()
        for t in range(T):
            def put(at, value, t=t, q=q):
                other = recv_d1[q, t, pl.ds(at, step), :].astype(F32)
                send_d2[q, t, pl.ds(at, step), :] = (value + other).astype(BF16)
            combine(col_of, goal * T + t, put)
        d2[q] = remote(send_d2.at[q], recv_d2.at[q], d2_send.at[q], d2_recv.at[q], (goal, r))
        d2[q].start()

    scale = 1.0 / (n * R)
    for s in range(1, n):
        w2[s].wait_recv()
    summed = recv_w2[0]
    for j in range(1, n):
        summed = summed + recv_w2[j]
    bgrad_out[...] = jnp.sum(summed[cb:, :], axis=0, keepdims=True) * scale
    slab_w3[b] = summed[:cb, :] * scale
    w3 = {}
    for s in range(1, n):
        w3[s] = remote(slab_w3.at[b], slab_w3.at[b], w3_send.at[s], w3_recv.at[s], (flip(b, s), r))
        w3[s].start()

    d1[0].wait_recv()
    for s in range(1, n):
        w3[s].wait_recv()
    for j in range(n):
        slab_w4[r, j * fb:(j + 1) * fb, :] = slab_w3[j, :fb, :]
    w4 = {}
    for s in peers:
        w4[s] = remote(slab_w4.at[r], slab_w4.at[r], w4_send.at[s], w4_recv.at[s], (b, flip(r, s)))
        w4[s].start()

    for q in far:
        d2[q].wait_recv()
    for t in range(T):
        def put(at, value, t=t):
            value = value + recv_d1[0, t, pl.ds(at, step), :].astype(F32)
            for q in far:
                value = value + recv_d2[q, t, pl.ds(at, step), :].astype(F32)
            fgrad_out[pl.ds(t * size + at, step), :] = value.astype(BF16)
        combine(col_of, b * T + t, put)

    for s in peers:
        w4[s].wait_recv()
    for q in range(R):
        wgrad_out[q * fr:(q + 1) * fr, :] = slab_w4[q]

    for group in (az[1:], ay, bs.values(), cs.values(), d1.values(), d2.values(),
                  w1.values(), w2.values(), w3.values(), w4.values()):
        for c in group:
            c.wait_send()


def per_device(n, R, features, tiles, tile_rows, tile_cols, counts, weight, bias, cotangent):
    own_rows, width = features.shape
    S, size = tiles.shape[1], tiles.shape[2]
    T = own_rows // size
    half = n // 2
    fr = weight.shape[0] // R
    fb = fr // n
    cb = max(8, fb)
    any_spec = pl.BlockSpec(memory_space=pl.ANY)
    smem = pl.BlockSpec(memory_space=pltpu.SMEM)
    vmem = pl.BlockSpec(memory_space=pltpu.VMEM)
    block = (T, size, width)
    dma = pltpu.SemaphoreType.DMA
    scratch = [
        pltpu.VMEM((n * T, size, width), BF16),
        pltpu.VMEM((S, size, size), BF16),
        pltpu.VMEM(weight.shape, BF16),
        pltpu.VMEM((own_rows, width), BF16),
        pltpu.VMEM((S, size, width), F32),
        pltpu.VMEM((R,) + block, BF16),
        pltpu.VMEM((R,) + block, BF16),
        pltpu.VMEM((R * T, size, width), BF16),
    ] + [pltpu.VMEM((half,) + block, BF16)] * 4 + [
        pltpu.VMEM((R, fr + 8, width), F32),
        pltpu.VMEM((R, fr + 8, width), F32),
        pltpu.VMEM((n, cb + 8, width), F32),
        pltpu.VMEM((n, cb + 8, width), F32),
        pltpu.VMEM((n, cb, width), F32),
        pltpu.VMEM((R, fr, width), F32),
        dma((4,)),
    ] + [dma((half,))] * 4 + [dma((R,))] * 4 + [dma((half,))] * 4 + [
        dma((R,)), dma((R,)), dma((n,)), dma((n,)), dma((n,)), dma((n,)), dma((R,)), dma((R,)),
    ]
    act, fgrad, wgrad, bgrad = pl.pallas_call(
        functools.partial(kernel, n, R, T, S),
        out_shape=(
            jax.ShapeDtypeStruct((own_rows, width), BF16),
            jax.ShapeDtypeStruct((own_rows, width), BF16),
            jax.ShapeDtypeStruct(weight.shape, F32),
            jax.ShapeDtypeStruct((1, width), F32),
        ),
        in_specs=[any_spec, any_spec, smem, smem, smem, any_spec, vmem, any_spec],
        out_specs=(vmem, vmem, vmem, vmem),
        scratch_shapes=scratch,
        compiler_params=pltpu.CompilerParams(
            collective_id=0, has_side_effects=True, vmem_limit_bytes=48 * 1024 * 1024),
        name="graph_layer",
    )(features.reshape(block), tiles[0], tile_rows, tile_cols, counts, weight,
      bias.reshape(1, -1), cotangent)
    return act, fgrad, wgrad, bgrad[0]


def solution(mesh):
    in_specs = (
        P(("blk", "rep"), None),
        P("blk", "rep", None, None),
        P("blk", "rep"),
        P("blk", "rep"),
        P("blk", "rep"),
        P(),
        P(),
        P(("blk", "rep"), None),
    )
    out_specs = (P(("blk", "rep"), None), P(("blk", "rep"), None), P(), P())
    body = functools.partial(per_device, mesh.shape["blk"], mesh.shape["rep"])
    return jax.shard_map(body, mesh=mesh, in_specs=in_specs, out_specs=out_specs, check_vma=False)
```

time: 243 us -> 71 us (0.29)
  waiting for transfers between devices: 145 us -> 0 us
  Pallas kernels: 0 us -> 62.4 us
  blocking collectives: 43.5 us -> 0 us
  matrix products: 16.7 us -> 0 us
  between operations: 14.6 us -> 1.32 us
  local copies, waits for them, and re-layouts: 16.3 us -> 7 us
  other arithmetic: 4.1 us -> 0 us
    ppermute x8 -> x0, waiting for transfers between devices: 76.8 us -> none  [shifted(): return lax.ppermute(block, axis, route)]
    pallas_call x0 -> x1, Pallas kernels: none -> 62.4 us  [per_device(): pl.pallas_call(functools.partial(kernel, n, R, T, S), out_shape=(jax.Shap...]
    all_gather x1 -> x0, waiting for transfers between devices: 43.7 us -> none  [per_device(): piece = lax.all_gather(features, 'blk', axis=0, tiled=True)]
    psum x1 -> x0, blocking collectives: 36.9 us -> none  [per_device(): lax.psum((local_weight, local_bias), ('blk', 'rep'))]
    reduce_scatter x1 -> x0, waiting for transfers between devices: 23.6 us -> none  [per_device(): lax.psum_scatter(summed.reshape(rep_count * own_rows, feat_width), 'rep',...]
    dot_general x14 -> x0, matrix products: 16.7 us -> none  [the longest x8 6.57 us: column_terms(): jnp.einsum('sp,sjf->pjf', col_onehot, contribution, precision=highest)]
    gather x2 -> x0, local copies, waits for them, and re-layouts: 10.4 us -> none  [the longest x1 9.83 us: per_device(): jnp.take(piece, clipped.reshape(-1), axis=0)]
    unnamed x14 -> x18, local copies, waits for them, and re-layouts: 0.04 us -> 7 us
  transfers between devices with their start and end apart: 11 -> 0, of which waited for: 10 -> 0; matrix products, arithmetic and copies ran while one was open for 6% -> 0% of each run, Pallas kernels for 0% -> 0%
where the time goes in v1:
time: 71 us; the launch traced here: 70.7 us
  Pallas kernels  62.4 us (88%)
  local copies, waits for them, and re-layouts  7 us (10%)
  between operations  1.32 us (2%)
    pallas_call x1, Pallas kernels, per_device(): pl.pallas_call(functools.partial(kernel, n, R, T, S), out_shape=(jax.Shap...  62.4 us
    unnamed x18, local copies, waits for them, and re-layouts  7 us

profile of v1, /device:TPU:0, one launch (start us, length us, event | category | flops | bytes accessed | tf_op | source)
XLA Modules:
  0.0 70.7 jit_solution(7116626661569770183)
XLA Ops:
  1.3 0.0 copy-start.6
  1.3 0.0 copy-start.4
  1.3 0.0 copy-start.5
  1.3 0.6 copy-done.6
  1.9 0.0 copy-done.4
  2.0 0.0 copy-done.5
  2.0 0.0 copy-start
  2.0 1.0 %copy-done = bf16[1,16,128,128]{3,2,1,0:T(8,128)(2,1)S(1)} copy-done((bf16[1,16,128,128]{3,2,1,0:T(8,128)(2,1)S(1)}, bf16[1,16,128,128]{3,2,1,0:T(8,128)(2,1)}, u32[]{:S(2)}) %copy-start) | copy-done | bytes 524312
  3.0 0.0 copy-start.1
  3.0 0.9 %copy-done.1 = bf16[256,256]{1,0:T(8,128)(2,1)S(1)} copy-done((bf16[256,256]{1,0:T(8,128)(2,1)S(1)}, bf16[256,256]{1,0:T(8,128)(2,1)}, u32[]{:S(2)}) %copy-start.1) | copy-done | bytes 131096
  3.9 0.0 copy-start.2
  3.9 0.9 %copy-done.2 = bf16[256,256]{1,0:T(8,128)(2,1)S(1)} copy-done((bf16[256,256]{1,0:T(8,128)(2,1)S(1)}, bf16[256,256]{1,0:T(8,128)(2,1)}, u32[]{:S(2)}) %copy-start.2) | copy-done | bytes 131096
  4.8 0.0 copy-start.3
  4.8 0.9 %copy-done.3 = bf16[256,256]{1,0:T(8,128)(2,1)S(1)} copy-done((bf16[256,256]{1,0:T(8,128)(2,1)S(1)}, bf16[256,256]{1,0:T(8,128)(2,1)}, u32[]{:S(2)}) %copy-start.3) | copy-done | bytes 131096
  5.7 62.4 %graph_layer.1 = (bf16[256,256]{1,0:T(8,128)(2,1)S(1)}, bf16[256,256]{1,0:T(8,128)(2,1)S(1)}, f32[256,256]{1,0:T(8,128)S(1)}, f32[1,256]{1,0:T(1,128)S(1)}) custom-call(bf16[2,128,256]{2,1,0:T(8,128)(2,1)S(1)} %bitcast.5, bf16[16,128,128]{2,1,0:T(8,128)(2,1)S(1)} %bitcast.4, s32[1,16]{1,0:T(1,128)S(1)} %copy-done.5, s32[1,16]{1,0:T(1,128)S(1)} %copy-done.6, ...), custom_call_target="tpu_custom_call" | custom-call | tf_op jit(solution)/shard_map/graph_layer/pallas_call | solution.py:275
  68.2 0.7 copy.17
  68.8 0.7 copy.18
  69.5 0.7 copy.19
  70.2 0.6 copy.20
Async XLA Ops:
  1.3 0.7 copy-start.6
  1.3 0.7 copy-start.4
  1.3 0.7 copy-start.5
  2.0 1.0 %copy-start = (bf16[1,16,128,128]{3,2,1,0:T(8,128)(2,1)S(1)}, bf16[1,16,128,128]{3,2,1,0:T(8,128)(2,1)}, u32[]{:S(2)}) copy-start(bf16[1,16,128,128]{3,2,1,0:T(8,128)(2,1)} %param.9) | copy-start | bytes 1572868
  3.0 0.9 %copy-start.1 = (bf16[256,256]{1,0:T(8,128)(2,1)S(1)}, bf16[256,256]{1,0:T(8,128)(2,1)}, u32[]{:S(2)}) copy-start(bf16[256,256]{1,0:T(8,128)(2,1)} %param.8) | copy-start | bytes 393220
  3.9 0.9 %copy-start.2 = (bf16[256,256]{1,0:T(8,128)(2,1)S(1)}, bf16[256,256]{1,0:T(8,128)(2,1)}, u32[]{:S(2)}) copy-start(bf16[256,256]{1,0:T(8,128)(2,1)} %weight.1) | copy-start | bytes 393220
  4.8 0.9 %copy-start.3 = (bf16[256,256]{1,0:T(8,128)(2,1)S(1)}, bf16[256,256]{1,0:T(8,128)(2,1)}, u32[]{:S(2)}) copy-start(bf16[256,256]{1,0:T(8,128)(2,1)} %cotangent.1) | copy-start | bytes 393220

commit v2 on v1

v2 whole, which is shorter than its diff:
```python
import functools

import jax
import jax.numpy as jnp
from jax import lax
from jax.experimental import pallas as pl
from jax.experimental.pallas import tpu as pltpu
from jax.sharding import PartitionSpec as P

MESH = pl.DeviceIdType.MESH
F32 = jnp.float32
BF16 = jnp.bfloat16
VMEM_LIMIT = 63 * 1024 * 1024


def flip(index, bits):
    out = index
    bit = 1
    while bit <= bits:
        if bits & bit:
            out = out + bit - 2 * bit * ((index // bit) % 2)
        bit *= 2
    return out


def kernel(n, R, T, S, features, tiles, rows_in, cols_in, counts_in, weight, bias_in, cotangent,
           act_out, fgrad_out, wgrad_out, bgrad_out,
           rows, cols, counts, bias, feat, tile_v, weight_v, cot_v, prod, send_b, recv_b, grads,
           send_d1, recv_d1, send_d2, recv_d2,
           send_w1, recv_w1, send_w2, recv_w2, slab_w3, slab_w4,
           load_sem, az_send, az_recv, ay_send, ay_recv, b_send, b_recv, c_send, c_recv,
           d1_send, d1_recv, d2_send, d2_recv, w1_send, w1_recv, w2_send, w2_recv,
           w3_send, w3_recv, w4_send, w4_recv):
    b = lax.axis_index("blk")
    r = lax.axis_index("rep")
    half = n // 2
    size = tiles.shape[1]
    width = weight.shape[1]
    fb = weight.shape[0] // n
    fr = fb // R
    cb = send_w1.shape[1] - 16
    cr = send_w2.shape[1] - 8
    partner = flip(b, 1)

    def remote(src, dst, ssem, rsem, device):
        return pltpu.make_async_remote_copy(
            src_ref=src, dst_ref=dst, send_sem=ssem, recv_sem=rsem,
            device_id=device, device_id_type=MESH)

    loads = [
        pltpu.make_async_copy(features, feat.at[pl.ds(b * T, T)], load_sem.at[0]),
        pltpu.make_async_copy(tiles, tile_v, load_sem.at[1]),
        pltpu.make_async_copy(weight, weight_v, load_sem.at[2]),
        pltpu.make_async_copy(cotangent, cot_v, load_sem.at[3]),
        pltpu.make_async_copy(rows_in, rows, load_sem.at[4]),
        pltpu.make_async_copy(cols_in, cols, load_sem.at[5]),
        pltpu.make_async_copy(counts_in, counts, load_sem.at[6]),
        pltpu.make_async_copy(bias_in, bias, load_sem.at[7]),
    ]
    for c in loads:
        c.start()

    barrier = pltpu.get_barrier_semaphore()
    for s in range(1, n):
        pl.semaphore_signal(barrier, inc=1, device_id=(flip(b, s), r), device_id_type=MESH)
    for s in range(1, R):
        pl.semaphore_signal(barrier, inc=1, device_id=(b, flip(r, s)), device_id_type=MESH)
    pl.semaphore_wait(barrier, n - 1 + R - 1)

    loads[0].wait()
    order = sorted(range(1, half), key=lambda q: (q.bit_count(), q))
    own = [feat.at[b * T + t] for t in range(T)]
    az, ay = {}, {}
    for t in range(T):
        ay[0, t] = remote(own[t], own[t], ay_send.at[0, t], ay_recv.at[0, t], (partner, r))
        ay[0, t].start()
    for q in order:
        for t in range(T):
            az[q, t] = remote(own[t], own[t], az_send.at[q, t], az_recv.at[q, t],
                              (flip(b, 2 * q), r))
            az[q, t].start()
    for q in order:
        for t in range(T):
            az[q, t].wait_recv()
            tile = feat.at[flip(b, 2 * q) * T + t]
            ay[q, t] = remote(tile, tile, ay_send.at[q, t], ay_recv.at[q, t], (partner, r))
            ay[q, t].start()
    for c in loads[1:]:
        c.wait()
    for q in [0] + order:
        for t in range(T):
            ay[q, t].wait_recv()

    live = [lax.convert_element_type(k < counts[0, 0], F32) for k in range(S)]
    row_of = [rows[0, k] for k in range(S)]
    col_of = [cols[0, k] for k in range(S)]

    for k in range(S):
        prod[k] = jnp.dot(tile_v[k], feat[col_of[k]], preferred_element_type=F32)

    step = 32

    def combine(index_of, target, dest):
        w = [jnp.where(index_of[k] == target, live[k], 0.0) for k in range(S)]

        def chunk(i, carry):
            at = pl.multiple_of(i * step, step)
            total = prod[0, pl.ds(at, step), :] * w[0]
            for k in range(1, S):
                total = total + prod[k, pl.ds(at, step), :] * w[k]
            dest(at, total)
            return carry

        lax.fori_loop(0, size // step, chunk, 0)

    bs = {}
    peers = sorted(range(1, R), key=lambda s: (-(s // 2), s))
    for s in peers:
        peer = flip(r, s)
        for t in range(T):
            def put(at, value, t=t, s=s):
                send_b[s, t, pl.ds(at, step), :] = value.astype(BF16)
            combine(row_of, peer * T + t, put)
        bs[s] = remote(send_b.at[s], recv_b.at[s], b_send.at[s], b_recv.at[s], (b, peer))
        bs[s].start()
    own_value = []
    for t in range(T):
        w = [jnp.where(row_of[k] == r * T + t, live[k], 0.0) for k in range(S)]
        total = prod[0] * w[0]
        for k in range(1, S):
            total = total + prod[k] * w[k]
        own_value.append(total)
    total = jnp.concatenate(own_value, axis=0)
    for s in peers[::-1]:
        bs[s].wait_recv()
        total = total + recv_b[s].reshape(T * size, width).astype(F32)
    agg = total.astype(BF16)
    pre = jnp.dot(agg, weight_v[...], preferred_element_type=F32) + bias[...]
    sig = jax.nn.sigmoid(pre)
    act_grad = (cot_v[...].astype(F32) * sig * (1.0 + pre * (1.0 - sig))).astype(BF16)
    grad = lax.dot_general(act_grad, weight_v[...], (((1,), (1,)), ((), ())),
                           preferred_element_type=F32).astype(BF16)
    here = grads.at[pl.ds(r * T, T)]
    grads[pl.ds(r * T, T)] = grad.reshape(T, size, width)
    cs = {}
    for s in peers:
        cs[s] = remote(here, here, c_send.at[s], c_recv.at[s], (b, flip(r, s)))
        cs[s].start()

    part = lax.dot_general(agg, act_grad, (((0,), (0,)), ((), ())), preferred_element_type=F32)
    bias_part = jnp.sum(act_grad.astype(F32).reshape(-1, 16, width), axis=0).astype(BF16)
    part = part.astype(BF16)
    for q in range(n):
        send_w1[q, :fb, :] = part[q * fb:(q + 1) * fb, :]
        send_w1[q, cb:, :] = bias_part
    w1 = {}
    for s in range(1, n):
        peer = flip(b, s)
        w1[s] = remote(send_w1.at[peer], recv_w1.at[b], w1_send.at[s], w1_recv.at[s], (peer, r))
        w1[s].start()
    recv_w1[b] = send_w1[b]
    act_out[...] = (pre * sig).astype(BF16)

    for s in peers:
        cs[s].wait_recv()
    for k in range(S):
        prod[k] = lax.dot_general(tile_v[k], grads[row_of[k]], (((0,), (0,)), ((), ())),
                                  preferred_element_type=F32)

    far = order[::-1]
    d1, d2, w2, w3, w4 = {}, {}, {}, {}, {}

    def to_partner(q):
        goal = flip(partner, 2 * q)
        for t in range(T):
            def put(at, value, t=t, q=q):
                send_d1[q, t, pl.ds(at, step), :] = value.astype(BF16)
            combine(col_of, goal * T + t, put)
            d1[q, t] = remote(send_d1.at[q, t], recv_d1.at[q, t], d1_send.at[q, t],
                              d1_recv.at[q, t], (partner, r))
            d1[q, t].start()

    def to_owner(q):
        goal = flip(b, 2 * q)
        for t in range(T):
            def put(at, value, t=t, q=q):
                other = recv_d1[q, t, pl.ds(at, step), :].astype(F32)
                send_d2[q, t, pl.ds(at, step), :] = (value + other).astype(BF16)
            d1[q, t].wait_recv()
            combine(col_of, goal * T + t, put)
            d2[q, t] = remote(send_d2.at[q, t], recv_d2.at[q, t], d2_send.at[q, t],
                              d2_recv.at[q, t], (goal, r))
            d2[q, t].start()

    def weights_over_rep():
        for s in range(1, n):
            w1[s].wait_recv()
        total = recv_w1[0].astype(F32)
        for q in range(1, n):
            total = total + recv_w1[q].astype(F32)
        biases = total[cb:cb + 8, :] + total[cb + 8:, :]
        for j in range(R):
            send_w2[j, :fr, :] = total[j * fr:(j + 1) * fr, :]
            send_w2[j, cr:, :] = biases
        for s in peers:
            peer = flip(r, s)
            w2[s] = remote(send_w2.at[peer], recv_w2.at[r], w2_send.at[s], w2_recv.at[s],
                           (b, peer))
            w2[s].start()
        recv_w2[r] = send_w2[r]

    scale = 1.0 / (n * R)

    def weights_back():
        for s in peers:
            w2[s].wait_recv()
        total = recv_w2[0]
        for j in range(1, R):
            total = total + recv_w2[j]
        bgrad_out[...] = jnp.sum(total[cr:, :], axis=0, keepdims=True) * scale
        slab_w3[b] = total[:cr, :] * scale
        for s in range(1, n):
            w3[s] = remote(slab_w3.at[b], slab_w3.at[b], w3_send.at[s], w3_recv.at[s],
                           (flip(b, s), r))
            w3[s].start()

    to_partner(far[0])
    weights_over_rep()
    for q in far[1:]:
        to_partner(q)
    weights_back()
    to_partner(0)
    for q in far:
        to_owner(q)

    for s in range(1, n):
        w3[s].wait_recv()
    for s in peers:
        w4[s] = remote(slab_w3, slab_w4.at[r], w4_send.at[s], w4_recv.at[s], (b, flip(r, s)))
        w4[s].start()
    slab_w4[r] = slab_w3[...]

    for t in range(T):
        d1[0, t].wait_recv()
        for q in far:
            d2[q, t].wait_recv()

        def put(at, value, t=t):
            value = value + recv_d1[0, t, pl.ds(at, step), :].astype(F32)
            for q in far:
                value = value + recv_d2[q, t, pl.ds(at, step), :].astype(F32)
            fgrad_out[pl.ds(t * size + at, step), :] = value.astype(BF16)
        combine(col_of, b * T + t, put)

    for s in peers:
        w4[s].wait_recv()
    for j in range(n):
        for q in range(R):
            wgrad_out[j * fb + q * fr:j * fb + (q + 1) * fr, :] = slab_w4[q, j, :fr, :]

    for group in (az.values(), ay.values(), bs.values(), cs.values(), d1.values(), d2.values(),
                  w1.values(), w2.values(), w3.values(), w4.values()):
        for c in group:
            c.wait_send()


def per_device(n, R, features, tiles, tile_rows, tile_cols, counts, weight, bias, cotangent):
    own_rows, width = features.shape
    S, size = tiles.shape[1], tiles.shape[2]
    T = own_rows // size
    half = n // 2
    fb = weight.shape[0] // n
    fr = fb // R
    cb, cr = max(16, fb), max(8, fr)
    hbm = pl.BlockSpec(memory_space=pltpu.HBM)
    vmem = pl.BlockSpec(memory_space=pltpu.VMEM)
    block = (T, size, width)
    dma = pltpu.SemaphoreType.DMA
    scratch = [
        pltpu.SMEM(tile_rows.shape, jnp.int32),
        pltpu.SMEM(tile_cols.shape, jnp.int32),
        pltpu.SMEM(counts.shape, jnp.int32),
        pltpu.VMEM((1, width), F32),
        pltpu.VMEM((n * T, size, width), BF16),
        pltpu.VMEM((S, size, size), BF16),
        pltpu.VMEM(weight.shape, BF16),
        pltpu.VMEM((own_rows, width), BF16),
        pltpu.VMEM((S, size, width), F32),
        pltpu.VMEM((R,) + block, BF16),
        pltpu.VMEM((R,) + block, BF16),
        pltpu.VMEM((R * T, size, width), BF16),
    ] + [pltpu.VMEM((half,) + block, BF16)] * 4 + [
        pltpu.VMEM((n, cb + 16, width), BF16),
        pltpu.VMEM((n, cb + 16, width), BF16),
        pltpu.VMEM((R, cr + 8, width), F32),
        pltpu.VMEM((R, cr + 8, width), F32),
        pltpu.VMEM((n, cr, width), F32),
        pltpu.VMEM((R, n, cr, width), F32),
        dma((8,)),
    ] + [dma((half, T))] * 4 + [dma((R,))] * 4 + [dma((half, T))] * 4 + [
        dma((n,)), dma((n,)), dma((R,)), dma((R,)), dma((n,)), dma((n,)), dma((R,)), dma((R,)),
    ]
    act, fgrad, wgrad, bgrad = pl.pallas_call(
        functools.partial(kernel, n, R, T, S),
        out_shape=(
            jax.ShapeDtypeStruct((own_rows, width), BF16),
            jax.ShapeDtypeStruct((own_rows, width), BF16),
            jax.ShapeDtypeStruct(weight.shape, F32),
            jax.ShapeDtypeStruct((1, width), F32),
        ),
        in_specs=[hbm] * 8,
        out_specs=(vmem, vmem, vmem, vmem),
        scratch_shapes=scratch,
        compiler_params=pltpu.CompilerParams(
            collective_id=0, has_side_effects=True, vmem_limit_bytes=VMEM_LIMIT),
        name="graph_layer",
    )(features.reshape(block), tiles[0], tile_rows, tile_cols, counts, weight,
      bias.reshape(1, -1), cotangent)
    return act, fgrad, wgrad, bgrad[0]


def solution(mesh):
    in_specs = (
        P(("blk", "rep"), None),
        P("blk", "rep", None, None),
        P("blk", "rep"),
        P("blk", "rep"),
        P("blk", "rep"),
        P(),
        P(),
        P(("blk", "rep"), None),
    )
    out_specs = (P(("blk", "rep"), None), P(("blk", "rep"), None), P(), P())
    body = functools.partial(per_device, mesh.shape["blk"], mesh.shape["rep"])
    return jax.shard_map(body, mesh=mesh, in_specs=in_specs, out_specs=out_specs, check_vma=False)
```

time: 71 us -> 61.5 us (0.87)
  Pallas kernels: 62.4 us -> 56.5 us
  local copies, waits for them, and re-layouts: 7 us -> 3.55 us
    pallas_call x1, Pallas kernels: 62.4 us -> 56.5 us  [per_device(): pl.pallas_call(functools.partial(kernel, n, R, T, S), out_shape=(jax.Shap...]
    unnamed x18 -> x10, local copies, waits for them, and re-layouts: 7 us -> 3.55 us
where the time goes in v2:
time: 61.5 us; the launch traced here: 61.3 us
  Pallas kernels  56.5 us (92%)
  local copies, waits for them, and re-layouts  3.55 us (6%)
  between operations  1.31 us (2%)
    pallas_call x1, Pallas kernels, per_device(): pl.pallas_call(functools.partial(kernel, n, R, T, S), out_shape=(jax.Shap...  56.5 us
    unnamed x10, local copies, waits for them, and re-layouts  3.55 us

profile of v2, /device:TPU:0, one launch (start us, length us, event | category | flops | bytes accessed | tf_op | source)
XLA Modules:
  0.0 61.3 jit_solution(1338175318203020533)
XLA Ops:
  1.3 56.5 %graph_layer.1 = (bf16[256,256]{1,0:T(8,128)(2,1)}, bf16[256,256]{1,0:T(8,128)(2,1)}, f32[256,256]{1,0:T(8,128)}, f32[1,256]{1,0:T(1,128)}) custom-call(bf16[2,128,256]{2,1,0:T(8,128)(2,1)} %bitcast.5, bf16[16,128,128]{2,1,0:T(8,128)(2,1)} %bitcast.4, s32[1,16]{1,0:T(1,128)} %rows_in.1, s32[1,16]{1,0:T(1,128)} %cols_in.1, s32[1,1]{1,0:T(1,128)S(6)} %copy.16.counts_in, ...), custom_call_target="tpu_custom_call" | custom-call | tf_op jit(solution)/shard_map/graph_layer/pallas_call | solution.py:303
  57.7 0.0 copy-start.1
  57.7 0.0 copy-start
  57.8 1.6 %copy.17 = bf16[256,256]{1,0:T(8,128)(2,1)} copy(bf16[256,256]{1,0:T(8,128)(2,1)} %get-tuple-element.16) | data formatting | bytes 262144
  59.4 0.0 copy-done.1
  59.4 0.7 %copy.18 = bf16[256,256]{1,0:T(8,128)(2,1)} copy(bf16[256,256]{1,0:T(8,128)(2,1)S(1)} %copy-done.1) | data formatting | bytes 262144
  60.0 0.0 copy-done
  60.0 0.0 copy-start.2
  60.0 0.7 %copy.19 = f32[256,256]{1,0:T(8,128)} copy(f32[256,256]{1,0:T(8,128)S(1)} %copy-done) | data formatting | bytes 524288
  60.7 0.0 copy-done.2
  60.7 0.6 copy.20
Async XLA Ops:
  57.7 1.6 %copy-start.1 = (bf16[256,256]{1,0:T(8,128)(2,1)S(1)}, bf16[256,256]{1,0:T(8,128)(2,1)}, u32[]{:S(2)}) copy-start(bf16[256,256]{1,0:T(8,128)(2,1)} %get-tuple-element.17) | copy-start | bytes 393220
  57.7 2.3 %copy-start = (f32[256,256]{1,0:T(8,128)S(1)}, f32[256,256]{1,0:T(8,128)}, u32[]{:S(2)}) copy-start(f32[256,256]{1,0:T(8,128)} %get-tuple-element.18) | copy-start | bytes 786436
  60.0 0.7 %copy-start.2 = (f32[1,256]{1,0:T(1,128)S(1)}, f32[1,256]{1,0:T(1,128)}, u32[]{:S(2)}) copy-start(f32[1,256]{1,0:T(1,128)} %get-tuple-element.11) | copy-start | bytes 3076

commit v3 on v2

--- a/solution.py
+++ b/solution.py
@@ -25,7 +25,7 @@
 
 def kernel(n, R, T, S, features, tiles, rows_in, cols_in, counts_in, weight, bias_in, cotangent,
            act_out, fgrad_out, wgrad_out, bgrad_out,
-           rows, cols, counts, bias, feat, tile_v, weight_v, cot_v, prod, send_b, recv_b, grads,
+           rows, cols, counts, bias, feat, tile_v, weight_v, cot_v, prod, total_v, send_b, recv_b, grads,
            send_d1, recv_d1, send_d2, recv_d2,
            send_w1, recv_w1, send_w2, recv_w2, slab_w3, slab_w4,
            load_sem, az_send, az_recv, ay_send, ay_recv, b_send, b_recv, c_send, c_recv,
@@ -113,39 +113,48 @@
 
         lax.fori_loop(0, size // step, chunk, 0)
 
-    bs = {}
+    bs, cs = {}, {}
     peers = sorted(range(1, R), key=lambda s: (-(s // 2), s))
-    for s in peers:
-        peer = flip(r, s)
-        for t in range(T):
+    for t in range(T):
+        for s in peers:
+            peer = flip(r, s)
+
             def put(at, value, t=t, s=s):
                 send_b[s, t, pl.ds(at, step), :] = value.astype(BF16)
+
             combine(row_of, peer * T + t, put)
-        bs[s] = remote(send_b.at[s], recv_b.at[s], b_send.at[s], b_recv.at[s], (b, peer))
-        bs[s].start()
-    own_value = []
-    for t in range(T):
-        w = [jnp.where(row_of[k] == r * T + t, live[k], 0.0) for k in range(S)]
-        total = prod[0] * w[0]
-        for k in range(1, S):
-            total = total + prod[k] * w[k]
-        own_value.append(total)
-    total = jnp.concatenate(own_value, axis=0)
-    for s in peers[::-1]:
-        bs[s].wait_recv()
-        total = total + recv_b[s].reshape(T * size, width).astype(F32)
-    agg = total.astype(BF16)
-    pre = jnp.dot(agg, weight_v[...], preferred_element_type=F32) + bias[...]
-    sig = jax.nn.sigmoid(pre)
-    act_grad = (cot_v[...].astype(F32) * sig * (1.0 + pre * (1.0 - sig))).astype(BF16)
-    grad = lax.dot_general(act_grad, weight_v[...], (((1,), (1,)), ((), ())),
-                           preferred_element_type=F32).astype(BF16)
-    here = grads.at[pl.ds(r * T, T)]
-    grads[pl.ds(r * T, T)] = grad.reshape(T, size, width)
-    cs = {}
-    for s in peers:
-        cs[s] = remote(here, here, c_send.at[s], c_recv.at[s], (b, flip(r, s)))
-        cs[s].start()
+            bs[s, t] = remote(send_b.at[s, t], recv_b.at[s, t], b_send.at[s, t],
+                              b_recv.at[s, t], (b, peer))
+            bs[s, t].start()
+    for t in range(T):
+
+        def put(at, value, t=t):
+            total_v[t, pl.ds(at, step), :] = value
+
+        combine(row_of, r * T + t, put)
+    agg_parts, act_parts = [], []
+    for t in range(T):
+        total = total_v[t]
+        for s in peers[::-1]:
+            bs[s, t].wait_recv()
+            total = total + recv_b[s, t].astype(F32)
+        agg_t = total.astype(BF16)
+        pre = jnp.dot(agg_t, weight_v[...], preferred_element_type=F32) + bias[...]
+        sig = jax.nn.sigmoid(pre)
+        cot_t = cot_v[t * size:(t + 1) * size, :].astype(F32)
+        act_t = (cot_t * sig * (1.0 + pre * (1.0 - sig))).astype(BF16)
+        grads[r * T + t] = lax.dot_general(
+            act_t, weight_v[...], (((1,), (1,)), ((), ())),
+            preferred_element_type=F32).astype(BF16)
+        here = grads.at[r * T + t]
+        for s in peers:
+            cs[s, t] = remote(here, here, c_send.at[s, t], c_recv.at[s, t], (b, flip(r, s)))
+            cs[s, t].start()
+        act_out[t * size:(t + 1) * size, :] = (pre * sig).astype(BF16)
+        agg_parts.append(agg_t)
+        act_parts.append(act_t)
+    agg = jnp.concatenate(agg_parts, axis=0)
+    act_grad = jnp.concatenate(act_parts, axis=0)
 
     part = lax.dot_general(agg, act_grad, (((0,), (0,)), ((), ())), preferred_element_type=F32)
     bias_part = jnp.sum(act_grad.astype(F32).reshape(-1, 16, width), axis=0).astype(BF16)
@@ -159,10 +168,10 @@
         w1[s] = remote(send_w1.at[peer], recv_w1.at[b], w1_send.at[s], w1_recv.at[s], (peer, r))
         w1[s].start()
     recv_w1[b] = send_w1[b]
-    act_out[...] = (pre * sig).astype(BF16)
-
-    for s in peers:
-        cs[s].wait_recv()
+
+    for t in range(T):
+        for s in peers:
+            cs[s, t].wait_recv()
     for k in range(S):
         prod[k] = lax.dot_general(tile_v[k], grads[row_of[k]], (((0,), (0,)), ((), ())),
                                   preferred_element_type=F32)
@@ -262,6 +271,13 @@
                   w1.values(), w2.values(), w3.values(), w4.values()):
         for c in group:
             c.wait_send()
+
+
+def emit(a, f, w, g, a_out, f_out, w_out, g_out):
+    a_out[...] = a[...]
+    f_out[...] = f[...]
+    w_out[...] = w[...]
+    g_out[...] = g[...]
 
 
 def per_device(n, R, features, tiles, tile_rows, tile_cols, counts, weight, bias, cotangent):
@@ -286,6 +302,7 @@
         pltpu.VMEM(weight.shape, BF16),
         pltpu.VMEM((own_rows, width), BF16),
         pltpu.VMEM((S, size, width), F32),
+        pltpu.VMEM(block, F32),
         pltpu.VMEM((R,) + block, BF16),
         pltpu.VMEM((R,) + block, BF16),
         pltpu.VMEM((R * T, size, width), BF16),
@@ -297,7 +314,7 @@
         pltpu.VMEM((n, cr, width), F32),
         pltpu.VMEM((R, n, cr, width), F32),
         dma((8,)),
-    ] + [dma((half, T))] * 4 + [dma((R,))] * 4 + [dma((half, T))] * 4 + [
+    ] + [dma((half, T))] * 4 + [dma((R, T))] * 4 + [dma((half, T))] * 4 + [
         dma((n,)), dma((n,)), dma((R,)), dma((R,)), dma((n,)), dma((n,)), dma((R,)), dma((R,)),
     ]
     act, fgrad, wgrad, bgrad = pl.pallas_call(
@@ -316,7 +333,15 @@
         name="graph_layer",
     )(features.reshape(block), tiles[0], tile_rows, tile_cols, counts, weight,
       bias.reshape(1, -1), cotangent)
-    return act, fgrad, wgrad, bgrad[0]
+    results = pl.pallas_call(
+        emit,
+        out_shape=tuple(jax.ShapeDtypeStruct(x.shape, x.dtype)
+                        for x in (act, fgrad, wgrad, bgrad)),
+        in_specs=[vmem] * 4,
+        out_specs=(vmem,) * 4,
+        name="emit_results",
+    )(act, fgrad, wgrad, bgrad)
+    return results[0], results[1], results[2], results[3][0]
 
 
 def solution(mesh):

time: 61.5 us -> 58.6 us (0.953)
  local copies, waits for them, and re-layouts: 3.55 us -> 0 us
  Pallas kernels: 56.5 us -> 57.2 us
    unnamed x10 -> x0, local copies, waits for them, and re-layouts: 3.55 us -> none
    pallas_call x0 -> x1, Pallas kernels: none -> 1.89 us  [per_device(): pl.pallas_call(emit, out_shape=tuple((jax.ShapeDtypeStruct(x.shape, x.dty...]
    pallas_call x1, Pallas kernels: 56.5 us -> 55.3 us  [per_device(): pl.pallas_call(functools.partial(kernel, n, R, T, S), out_shape=(jax.Shap...]
where the time goes in v3:
time: 58.6 us; the launch traced here: 58.5 us
  Pallas kernels  57.2 us (98%)
  between operations  1.29 us (2%)
    pallas_call x1, Pallas kernels, per_device(): pl.pallas_call(functools.partial(kernel, n, R, T, S), out_shape=(jax.Shap...  55.3 us
    pallas_call x1, Pallas kernels, per_device(): pl.pallas_call(emit, out_shape=tuple((jax.ShapeDtypeStruct(x.shape, x.dty...  1.89 us

profile of v3, /device:TPU:0, one launch (start us, length us, event | category | flops | bytes accessed | tf_op | source)
XLA Modules:
  0.0 58.5 jit_solution(5959712489419094246)
XLA Ops:
  1.3 55.3 %graph_layer.1 = (bf16[256,256]{1,0:T(8,128)(2,1)}, bf16[256,256]{1,0:T(8,128)(2,1)}, f32[256,256]{1,0:T(8,128)}, f32[1,256]{1,0:T(1,128)}) custom-call(bf16[2,128,256]{2,1,0:T(8,128)(2,1)} %bitcast.5, bf16[16,128,128]{2,1,0:T(8,128)(2,1)} %bitcast.4, s32[1,16]{1,0:T(1,128)} %rows_in.1, s32[1,16]{1,0:T(1,128)} %cols_in.1, s32[1,1]{1,0:T(1,128)S(6)} %copy.12.counts_in, ...), custom_call_target="tpu_custom_call" | custom-call | tf_op jit(solution)/shard_map/graph_layer/pallas_call | solution.py:320
  56.6 1.9 %emit_results.1 = (bf16[256,256]{1,0:T(8,128)(2,1)}, bf16[256,256]{1,0:T(8,128)(2,1)}, f32[256,256]{1,0:T(8,128)}, f32[1,256]{1,0:T(1,128)}) custom-call(bf16[256,256]{1,0:T(8,128)(2,1)} %get-tuple-element.12.a, bf16[256,256]{1,0:T(8,128)(2,1)} %get-tuple-element.13.f, f32[256,256]{1,0:T(8,128)} %get-tuple-element.14.w, f32[1,256]{1,0:T(1,128)} %get-tuple-element.15.g), custom_call_target="tpu_custom_call" | custom-call | tf_op jit(solution)/shard_map/emit_results/pallas_call | solution.py:336

commit v4 on v3

--- a/solution.py
+++ b/solution.py
@@ -147,7 +147,7 @@
             act_t, weight_v[...], (((1,), (1,)), ((), ())),
             preferred_element_type=F32).astype(BF16)
         here = grads.at[r * T + t]
-        for s in peers:
+        for s in [s for s in peers if s % 2 == 0] + [1]:
             cs[s, t] = remote(here, here, c_send.at[s, t], c_recv.at[s, t], (b, flip(r, s)))
             cs[s, t].start()
         act_out[t * size:(t + 1) * size, :] = (pre * sig).astype(BF16)
@@ -171,7 +171,16 @@
 
     for t in range(T):
         for s in peers:
-            cs[s, t].wait_recv()
+            if s % 2 == 0:
+                cs[s, t].wait_recv()
+                block = grads.at[flip(r, s) * T + t]
+                cs[s + 1, t] = remote(block, block, c_send.at[s + 1, t], c_recv.at[s + 1, t],
+                                      (b, flip(r, 1)))
+                cs[s + 1, t].start()
+    for t in range(T):
+        for s in peers:
+            if s % 2 == 1:
+                cs[s, t].wait_recv()
     for k in range(S):
         prod[k] = lax.dot_general(tile_v[k], grads[row_of[k]], (((0,), (0,)), ((), ())),
                                   preferred_element_type=F32)

time: 58.6 us -> 58.2 us (level)
  no operation moved by 1% of the time
where the time goes in v4:
time: 58.2 us; the launch traced here: 58 us
  Pallas kernels  56.7 us (97%)
  between operations  1.29 us (2%)
    pallas_call x1, Pallas kernels, per_device(): pl.pallas_call(functools.partial(kernel, n, R, T, S), out_shape=(jax.Shap...  54.8 us
    pallas_call x1, Pallas kernels, per_device(): pl.pallas_call(emit, out_shape=tuple((jax.ShapeDtypeStruct(x.shape, x.dty...  1.89 us

profile of v4, /device:TPU:0, one launch (start us, length us, event | category | flops | bytes accessed | tf_op | source)
XLA Modules:
  0.0 58.0 jit_solution(6152163982877230123)
XLA Ops:
  1.3 54.8 %graph_layer.1 = (bf16[256,256]{1,0:T(8,128)(2,1)}, bf16[256,256]{1,0:T(8,128)(2,1)}, f32[256,256]{1,0:T(8,128)}, f32[1,256]{1,0:T(1,128)}) custom-call(bf16[2,128,256]{2,1,0:T(8,128)(2,1)} %bitcast.5, bf16[16,128,128]{2,1,0:T(8,128)(2,1)} %bitcast.4, s32[1,16]{1,0:T(1,128)} %rows_in.1, s32[1,16]{1,0:T(1,128)} %cols_in.1, s32[1,1]{1,0:T(1,128)S(6)} %copy.12.counts_in, ...), custom_call_target="tpu_custom_call" | custom-call | tf_op jit(solution)/shard_map/graph_layer/pallas_call | solution.py:329
  56.1 1.9 %emit_results.1 = (bf16[256,256]{1,0:T(8,128)(2,1)}, bf16[256,256]{1,0:T(8,128)(2,1)}, f32[256,256]{1,0:T(8,128)}, f32[1,256]{1,0:T(1,128)}) custom-call(bf16[256,256]{1,0:T(8,128)(2,1)} %get-tuple-element.12.a, bf16[256,256]{1,0:T(8,128)(2,1)} %get-tuple-element.13.f, f32[256,256]{1,0:T(8,128)} %get-tuple-element.14.w, f32[1,256]{1,0:T(1,128)} %get-tuple-element.15.g), custom_call_target="tpu_custom_call" | custom-call | tf_op jit(solution)/shard_map/emit_results/pallas_call | solution.py:345

commit v5 on v4

--- a/solution.py
+++ b/solution.py
@@ -185,7 +185,7 @@
         prod[k] = lax.dot_general(tile_v[k], grads[row_of[k]], (((0,), (0,)), ((), ())),
                                   preferred_element_type=F32)
 
-    far = order[::-1]
+    far = order
     d1, d2, w2, w3, w4 = {}, {}, {}, {}, {}
 
     def to_partner(q):

time: 58.2 us -> 56.9 us (0.978)
  Pallas kernels: 56.7 us -> 55.4 us
    pallas_call x1, Pallas kernels: 54.8 us -> 53.6 us  [per_device(): pl.pallas_call(functools.partial(kernel, n, R, T, S), out_shape=(jax.Shap...]
where the time goes in v5:
time: 56.9 us; the launch traced here: 56.7 us
  Pallas kernels  55.4 us (97%)
  between operations  1.29 us (2%)
    pallas_call x1, Pallas kernels, per_device(): pl.pallas_call(functools.partial(kernel, n, R, T, S), out_shape=(jax.Shap...  53.6 us
    pallas_call x1, Pallas kernels, per_device(): pl.pallas_call(emit, out_shape=tuple((jax.ShapeDtypeStruct(x.shape, x.dty...  1.89 us

profile of v5, /device:TPU:0, one launch (start us, length us, event | category | flops | bytes accessed | tf_op | source)
XLA Modules:
  0.0 56.7 jit_solution(15735768755187403614)
XLA Ops:
  1.3 53.6 %graph_layer.1 = (bf16[256,256]{1,0:T(8,128)(2,1)}, bf16[256,256]{1,0:T(8,128)(2,1)}, f32[256,256]{1,0:T(8,128)}, f32[1,256]{1,0:T(1,128)}) custom-call(bf16[2,128,256]{2,1,0:T(8,128)(2,1)} %bitcast.5, bf16[16,128,128]{2,1,0:T(8,128)(2,1)} %bitcast.4, s32[1,16]{1,0:T(1,128)} %rows_in.1, s32[1,16]{1,0:T(1,128)} %cols_in.1, s32[1,1]{1,0:T(1,128)S(6)} %copy.12.counts_in, ...), custom_call_target="tpu_custom_call" | custom-call | tf_op jit(solution)/shard_map/graph_layer/pallas_call | solution.py:329
  54.8 1.9 %emit_results.1 = (bf16[256,256]{1,0:T(8,128)(2,1)}, bf16[256,256]{1,0:T(8,128)(2,1)}, f32[256,256]{1,0:T(8,128)}, f32[1,256]{1,0:T(1,128)}) custom-call(bf16[256,256]{1,0:T(8,128)(2,1)} %get-tuple-element.12.a, bf16[256,256]{1,0:T(8,128)(2,1)} %get-tuple-element.13.f, f32[256,256]{1,0:T(8,128)} %get-tuple-element.14.w, f32[1,256]{1,0:T(1,128)} %get-tuple-element.15.g), custom_call_target="tpu_custom_call" | custom-call | tf_op jit(solution)/shard_map/emit_results/pallas_call | solution.py:345
